TPU v7x, 32 devices: a whole 2x2x4 slice. The times are simulated.
32 devices in a mesh: groups: 2 (over y), blk: 4 (over z), head: 4 (over x, core).
Axes of the slice: x: 2, y: 2, z: 4, core: 2. Of those that a mesh axis runs over, the one named last changes fastest.
Arguments:
- queries: bfloat16 [4, 4, 8192], P('groups', 'blk', 'head'), parts along dimension 0, may hold values from -4.5 to 4.5
- stored_cache_keys: bfloat16 [4, 2048, 1024], P('groups', 'blk', 'head'), parts along dimension 0, may hold values from -4.5 to 4.5
- stored_cache_values: bfloat16 [4, 2048, 1024], P('groups', 'blk', 'head'), parts along dimension 0, may hold values from -6 to 6
- out_weight: bfloat16 [8192, 8192], P('head', 'blk'), may hold values from -3 to 3
- lengths: int32 [4], P('groups'), parts along dimension 0, may hold values from 1024 to 2048
Outputs:
- projected: bfloat16 [4, 4, 8192], P('groups', 'head', 'blk'), parts along dimension 0
There are 2 independent parts, one for each index of `groups`. A program takes and returns all parts, laid end to end along the dimension named above; an argument that names none is the same for every part. Nothing has to cross between parts.
All inputs are finite; a program needn't handle non-finite values.
Results may differ from a plain program's by a relative error of at most 0.0056.
Values may be sent and summed in bfloat16 or wider, within the bound.
A program may use at most 64 MiB of HBM per device.

v0:
```python
import math
import jax
import jax.numpy as jnp
from jax import lax
from jax.sharding import PartitionSpec as P

REQUEST_COUNT = 2
QUERY_HEAD_COUNT = 64
KEY_VALUE_HEADS = 8
HEAD_DIMENSION = 128
masked_fill_value = -1e30


def body(queries, stored_cache_keys, stored_cache_values, out_weight, lengths):
    group_width = QUERY_HEAD_COUNT // KEY_VALUE_HEADS
    local_heads = stored_cache_keys.shape[2] // HEAD_DIMENSION
    query_heads = local_heads * group_width
    span = stored_cache_keys.shape[1]
    new_count = queries.shape[1] * lax.axis_size("blk")
    key_pos = lax.axis_index("blk") * span + jnp.arange(span, dtype=jnp.int32)
    score_scale = 1.0 / math.sqrt(HEAD_DIMENSION)
    piece = lax.all_gather(queries, "blk", axis=1, tiled=True)
    rows_count = piece.shape[1]
    query_pos = lengths[:, None] - new_count + jnp.arange(rows_count, dtype=jnp.int32)[None, :]
    sums_list = []
    maxima_list = []
    totals_list = []
    for request in range(REQUEST_COUNT):
        visible = (key_pos[None, :] <= query_pos[request][:, None])[:, None, :]
        parts_sum, parts_max, parts_total = ([], [], [])
        for kv_head in range(local_heads):
            block_query = piece[
                request,
                :,
                kv_head
                * group_width
                * HEAD_DIMENSION : (kv_head + 1)
                * group_width
                * HEAD_DIMENSION,
            ].reshape(rows_count, group_width, HEAD_DIMENSION)
            local_keys = stored_cache_keys[
                request, :, kv_head * HEAD_DIMENSION : (kv_head + 1) * HEAD_DIMENSION
            ]
            local_values = stored_cache_values[
                request, :, kv_head * HEAD_DIMENSION : (kv_head + 1) * HEAD_DIMENSION
            ]
            scores = (
                jnp.einsum(
                    "ngd,cd->ngc", block_query, local_keys, preferred_element_type=jnp.float32
                )
                * score_scale
            )
            block_max = jnp.max(jnp.where(visible, scores, masked_fill_value), axis=-1)
            weights = jnp.where(visible, jnp.exp(scores - block_max[..., None]), 0.0)
            parts_total.append(jnp.sum(weights, axis=-1))
            parts_max.append(block_max)
            weighted = jnp.einsum(
                "ngc,cd->ngd",
                weights.astype(jnp.bfloat16),
                local_values,
                preferred_element_type=jnp.float32,
            )
            parts_sum.append(weighted.reshape(rows_count, group_width * HEAD_DIMENSION))
        sums_list.append(jnp.concatenate(parts_sum, axis=1))
        maxima_list.append(jnp.concatenate(parts_max, axis=1))
        totals_list.append(jnp.concatenate(parts_total, axis=1))
    new_sums = jnp.stack(sums_list, axis=0)
    new_maxima = jnp.stack(maxima_list, axis=0)
    new_totals = jnp.stack(totals_list, axis=0)
    received = (
        lax.all_to_all(new_sums[None], "blk", split_axis=2, concat_axis=0, tiled=True),
        lax.all_to_all(new_maxima[None], "blk", split_axis=2, concat_axis=0, tiled=True),
        lax.all_to_all(new_totals[None], "blk", split_axis=2, concat_axis=0, tiled=True),
    )
    part_sums, part_max, part_totals = received
    blocks = part_sums.shape[0]
    own_rows = part_sums.shape[2]
    top = jnp.max(part_max, axis=0)
    factor = jnp.exp(part_max - top[None])
    overall = jnp.sum(factor * part_totals, axis=0)
    shaped = part_sums.reshape(blocks, REQUEST_COUNT, own_rows, query_heads, HEAD_DIMENSION)
    merged = jnp.sum(shaped * factor[..., None], axis=0) / overall[..., None]
    own_attention = merged.astype(jnp.bfloat16).reshape(
        REQUEST_COUNT, own_rows, query_heads * HEAD_DIMENSION
    )
    terms = jnp.einsum(
        "rnc,cd->rnd",
        lax.all_gather(own_attention, "blk", axis=1, tiled=True),
        out_weight,
        preferred_element_type=jnp.float32,
    )
    return lax.psum_scatter(terms, "head", scatter_dimension=1, tiled=True).astype(jnp.bfloat16)


def solution(mesh):
    placed = (
        P("groups", "blk", "head"),
        P("groups", "blk", "head"),
        P("groups", "blk", "head"),
        P("head", "blk"),
        P("groups"),
    )
    return jax.shard_map(
        body, mesh=mesh, in_specs=placed, out_specs=P("groups", "head", "blk"), check_vma=False
    )
```

profile of v0, /device:TPU:0, one launch (start us, length us, event | category | flops | bytes accessed | tf_op | source)
XLA Modules:
  0.0 82.9 jit_solution(6853491526789684254)
XLA Ops:
  0.0 0.7 broadcast_add_fusion
  0.7 0.1 iota_add_fusion.1
  0.7 15.0 %all_gather.6 = bf16[2,4,2048]{2,0,1:T(2,128)(2,1)S(1)} all-gather(bf16[2,1,2048]{2,0,1:T(2,128)(2,1)} %param.5), channel_id=1, replica_groups=mesh['groups'=2,'blk'=4,'head'=4] {'blk'}, dimensions={1}, use_global_device_ids=true | all-gather | bytes 40960 | tf_op jit(solution)/shard_map/all_gather | solution.py:22
  15.8 0.1 slice_reduce_fusion.3
  15.9 0.1 broadcast_compare_fusion.1
  16.0 1.1 %select_reduce_fusion.3 = (f32[4,8]{1,0:T(4,128)S(1)}, f32[4,8,512]{2,1,0:T(8,128)S(1)}) fusion(pred[4,512]{1,0:T(4,128)(4,1)S(1)} %get-tuple-element.13, bf16[2,512,256]{2,1,0:T(8,128)(2,1)} %param.6, bf16[1,4,8,128]{3,1,2,0:T(4,128)(2,1)S(1)} %bitcast.152), kind=kOutput, calls=%fused_computation.36 | convolution fusion | flops 4243424 | bytes 206976 | tf_op jit(solution)/shard_map/ngd,cd->ngc/dot_general | solution.py:48
  17.2 1.1 %select_reduce_fusion.1 = (f32[4,8]{1,0:T(4,128)S(1)}, f32[4,8,512]{2,1,0:T(8,128)S(1)}) fusion(pred[4,512]{1,0:T(4,128)(4,1)S(1)} %get-tuple-element.14, bf16[2,512,256]{2,1,0:T(8,128)(2,1)} %param.6, bf16[1,4,8,128]{3,1,2,0:T(4,128)(2,1)S(1)} %bitcast.151), kind=kOutput, calls=%fused_computation.32 | convolution fusion | flops 4243424 | bytes 206976 | tf_op jit(solution)/shard_map/ngd,cd->ngc/dot_general | solution.py:48
  18.3 1.1 %fusion.19 = (f32[4,8]{1,0:T(4,128)S(1)}, f32[4,8]{1,0:T(4,128)S(1)}, f32[4,8,512]{2,1,0:T(8,128)S(1)}) fusion(f32[4,8,512]{2,1,0:T(8,128)S(1)} %get-tuple-element.21, f32[4,8]{1,0:T(4,128)S(1)} %get-tuple-element.20, pred[4,512]{1,0:T(4,128)(4,1)S(1)} %get-tuple-element.13, bf16[2,512,256]{2,1,0:T(8,128)(2,1)} %param.6, ...), kind=kOutput, calls=%fused_computation.37 | convolution fusion | flops 4292544 | bytes 272768 | tf_op jit(solution)/shard_map/ngd,cd->ngc/dot_general | solution.py:48
  19.4 1.1 %fusion.23 = (f32[4,8]{1,0:T(4,128)S(1)}, f32[4,8]{1,0:T(4,128)S(1)}, f32[4,8,512]{2,1,0:T(8,128)S(1)}) fusion(f32[4,8,512]{2,1,0:T(8,128)S(1)} %get-tuple-element.18, f32[4,8]{1,0:T(4,128)S(1)} %get-tuple-element.17, pred[4,512]{1,0:T(4,128)(4,1)S(1)} %get-tuple-element.14, bf16[2,512,256]{2,1,0:T(8,128)(2,1)} %param.6, ...), kind=kOutput, calls=%fused_computation.41 | convolution fusion | flops 4292544 | bytes 272768 | tf_op jit(solution)/shard_map/ngd,cd->ngc/dot_general | solution.py:48
  20.6 0.1 maximum_bitcast_fusion.3
  20.7 0.6 copy.16
  21.3 4.6 %all-to-all-start.1 = ((f32[1,2,4,16]{3,1,0,2:T(2,128)}), f32[1,2,4,16]{3,1,0,2:T(2,128)S(1)}, u32[]{:S(2)}, u32[]{:S(2)}) async-start(f32[1,2,4,16]{3,1,0,2:T(2,128)} %copy.16), calls=%async_computation.1 | async-start | bytes 8192 | tf_op jit(solution)/shard_map/all_to_all | solution.py:72
  25.9 1.1 %convolution_bitcast_fusion.3 = f32[1,4,8,128]{3,2,1,0:T(8,128)S(1)} fusion(bf16[2,512,256]{2,1,0:T(8,128)(2,1)} %param.7, f32[4,8,512]{2,1,0:T(8,128)S(1)} %get-tuple-element.21, f32[4,8]{1,0:T(4,128)S(1)} %get-tuple-element.20, pred[4,512]{1,0:T(4,128)(4,1)S(1)} %get-tuple-element.13), kind=kOutput, calls=%fused_computation.9 | convolution fusion | flops 4243456 | bytes 215168 | tf_op jit(solution)/shard_map/ngc,cd->ngd/dot_general | solution.py:57
  27.0 1.1 %convolution_bitcast_fusion.1 = f32[1,4,8,128]{3,2,1,0:T(8,128)S(1)} fusion(bf16[2,512,256]{2,1,0:T(8,128)(2,1)} %param.7, f32[4,8,512]{2,1,0:T(8,128)S(1)} %get-tuple-element.18, f32[4,8]{1,0:T(4,128)S(1)} %get-tuple-element.17, pred[4,512]{1,0:T(4,128)(4,1)S(1)} %get-tuple-element.14), kind=kOutput, calls=%fused_computation.7 | convolution fusion | flops 4243456 | bytes 215168 | tf_op jit(solution)/shard_map/ngc,cd->ngd/dot_general | solution.py:57
  28.1 1.1 %convolution_bitcast_fusion.2 = f32[1,4,8,128]{3,2,1,0:T(8,128)S(1)} fusion(bf16[2,512,256]{2,1,0:T(8,128)(2,1)} %param.7, f32[4,8,512]{2,1,0:T(8,128)S(1)} %get-tuple-element.22, f32[4,8]{1,0:T(4,128)S(1)} %get-tuple-element.10, pred[4,512]{1,0:T(4,128)(4,1)S(1)} %get-tuple-element.13), kind=kOutput, calls=%fused_computation.8 | convolution fusion | flops 4243456 | bytes 215168 | tf_op jit(solution)/shard_map/ngc,cd->ngd/dot_general | solution.py:57
  29.2 0.2 fusion.21
  29.4 1.1 %convolution_bitcast_fusion = f32[1,4,8,128]{3,2,1,0:T(8,128)S(1)} fusion(bf16[2,512,256]{2,1,0:T(8,128)(2,1)} %param.7, f32[4,8,512]{2,1,0:T(8,128)S(1)} %get-tuple-element.19, f32[4,8]{1,0:T(4,128)S(1)} %get-tuple-element.12, pred[4,512]{1,0:T(4,128)(4,1)S(1)} %get-tuple-element.14), kind=kOutput, calls=%fused_computation.6 | convolution fusion | flops 4243456 | bytes 215168 | tf_op jit(solution)/shard_map/ngc,cd->ngd/dot_general | solution.py:57
  30.7 0.1 maximum_bitcast_fusion.5
  30.8 0.1 maximum_bitcast_fusion.6
  30.8 0.7 maximum_bitcast_fusion
  31.5 0.6 copy.20
  32.1 1.2 %dynamic-slice = u32[1]{0:T(128)} dynamic-slice(u32[32]{0:T(128)} %constant.21, u32[]{:T(128)S(6)} %add.33), dynamic_slice_sizes={1} | dynamic-slice | bytes 12
  33.4 0.0 all-to-all-done.1
  33.4 5.1 %all-to-all-start.2 = ((f32[1,2,4,16]{3,1,0,2:T(2,128)}), f32[1,2,4,16]{3,1,0,2:T(2,128)S(1)}, u32[]{:S(2)}, u32[]{:S(2)}) async-start(f32[1,2,4,16]{3,1,0,2:T(2,128)} %copy.20), calls=%async_computation.2 | async-start | bytes 8192 | tf_op jit(solution)/shard_map/all_to_all | solution.py:73
  38.5 5.5 %all-to-all-done.2 = f32[1,2,4,16]{3,1,0,2:T(2,128)S(1)} async-done(((f32[1,2,4,16]{3,1,0,2:T(2,128)}), f32[1,2,4,16]{3,1,0,2:T(2,128)S(1)}, u32[]{:S(2)}, u32[]{:S(2)}) %all-to-all-start.2) | async-done | bytes 544 | tf_op jit(solution)/shard_map/all_to_all | solution.py:73
  44.0 3.3 %all-to-all-start = ((f32[1,2,4,2048]{3,1,0,2:T(2,128)}), f32[1,2,4,2048]{3,1,0,2:T(2,128)S(1)}, u32[]{:S(2)}, u32[]{:S(2)}) async-start(f32[1,2,4,2048]{3,1,0,2:T(2,128)} %maximum_bitcast_fusion), calls=%async_computation | async-start | bytes 131072 | tf_op jit(solution)/shard_map/all_to_all | solution.py:71
  47.4 0.1 div.19
  47.4 0.1 mul.44
  47.6 5.5 %all-to-all-done = f32[1,2,4,2048]{3,1,0,2:T(2,128)S(1)} async-done(((f32[1,2,4,2048]{3,1,0,2:T(2,128)}), f32[1,2,4,2048]{3,1,0,2:T(2,128)S(1)}, u32[]{:S(2)}, u32[]{:S(2)}) %all-to-all-start) | async-done | bytes 65568 | tf_op jit(solution)/shard_map/all_to_all | solution.py:71
  53.1 13.1 %all_gather.7 = bf16[2,4,2048]{2,0,1:T(2,128)(2,1)S(1)} all-gather(bf16[2,1,2048]{2,0,1:T(2,128)(2,1)S(1)} %fusion.43), channel_id=1, replica_groups=mesh['groups'=2,'blk'=4,'head'=4] {'blk'}, dimensions={1}, use_global_device_ids=true | all-gather | bytes 40960 | tf_op jit(solution)/shard_map/all_gather | solution.py:88
  66.2 4.7 %fusion = f32[2,4,2048]{2,0,1:T(2,128)S(1)} fusion(bf16[2,4,2048]{2,0,1:T(2,128)(2,1)S(1)} %all_gather.7, bf16[2048,2048]{1,0:T(8,128)(2,1)} %param.8), kind=kOutput, calls=%fused_computation | convolution fusion | flops 67108864 | bytes 8486912 | tf_op jit(solution)/shard_map/rnc,cd->rnd/dot_general | solution.py:86
  71.0 10.7 %all-reduce = bf16[2,4,2048]{2,0,1:T(2,128)(2,1)S(1)} all-reduce(f32[2,4,2048]{2,0,1:T(2,128)S(1)} %fusion), channel_id=2, replica_groups=mesh['groups'=2,'blk'=4,'head'=4] {'head'}, use_global_device_ids=true, to_apply=%region_11.12.clone | all-reduce | flops 16384 | bytes 98304
  81.6 1.2 %dynamic-slice_convert_fusion = bf16[2,1,2048]{2,0,1:T(2,128)(2,1)} fusion(bf16[2,4,2048]{2,0,1:T(2,128)(2,1)S(1)} %all-reduce, u32[]{:T(128)} %bitcast.39), kind=kLoop, calls=%fused_computation.67 | loop fusion | bytes 16388 | tf_op jit(solution)/shard_map/convert_element_type | solution.py:92
  (21 shorter events, 0.3 us)
Async XLA Ops:
  21.3 12.1 %all-to-all-start.1 = ((f32[1,2,4,16]{3,1,0,2:T(2,128)}), f32[1,2,4,16]{3,1,0,2:T(2,128)S(1)}, u32[]{:S(2)}, u32[]{:S(2)}) async-start(f32[1,2,4,16]{3,1,0,2:T(2,128)} %copy.16), calls=%async_computation.1 | async-start | bytes 8192 | tf_op jit(solution)/shard_map/all_to_all | solution.py:72
  33.4 10.7 %all-to-all-start.2 = ((f32[1,2,4,16]{3,1,0,2:T(2,128)}), f32[1,2,4,16]{3,1,0,2:T(2,128)S(1)}, u32[]{:S(2)}, u32[]{:S(2)}) async-start(f32[1,2,4,16]{3,1,0,2:T(2,128)} %copy.20), calls=%async_computation.2 | async-start | bytes 8192 | tf_op jit(solution)/shard_map/all_to_all | solution.py:73
  44.0 9.0 %all-to-all-start = ((f32[1,2,4,2048]{3,1,0,2:T(2,128)}), f32[1,2,4,2048]{3,1,0,2:T(2,128)S(1)}, u32[]{:S(2)}, u32[]{:S(2)}) async-start(f32[1,2,4,2048]{3,1,0,2:T(2,128)} %maximum_bitcast_fusion), calls=%async_computation | async-start | bytes 131072 | tf_op jit(solution)/shard_map/all_to_all | solution.py:71
where the time goes:
time: 83.4 us; the launch traced here: 82.9 us
  blocking collectives  38.8 us (47%)
  matrix products  13.7 us (16%)
  starting transfers between devices  13 us (16%)
  waiting for transfers between devices  11 us (13%)
  local copies, waits for them, and re-layouts  4.11 us (5%)
  other arithmetic  2.04 us (2%)
    all_gather x1, blocking collectives, body(): piece = lax.all_gather(queries, 'blk', axis=1, tiled=True)  15 us
    all_gather x1, blocking collectives, body(): lax.all_gather(own_attention, 'blk', axis=1, tiled=True)  13.1 us
    unnamed x1, blocking collectives  10.7 us
    all_to_all x1, waiting for transfers between devices, body(): lax.all_to_all(new_totals[None], 'blk', split_axis=2, concat_axis=0, tile...  5.54 us
    all_to_all x1, waiting for transfers between devices, body(): lax.all_to_all(new_sums[None], 'blk', split_axis=2, concat_axis=0, tiled=...  5.46 us
    all_to_all x1, starting transfers between devices, body(): lax.all_to_all(new_totals[None], 'blk', split_axis=2, concat_axis=0, tile...  5.09 us
    dot_general x1, matrix products, body(): jnp.einsum('rnc,cd->rnd', lax.all_gather(own_attention, 'blk', axis=1, ti...  4.71 us
    all_to_all x1, starting transfers between devices, body(): lax.all_to_all(new_maxima[None], 'blk', split_axis=2, concat_axis=0, tile...  4.63 us
  transfers between devices with their start and end apart: 3, of which 2 were waited for; matrix products, arithmetic and copies ran while one was open for 9% of the time, Pallas kernels for 0%

commit v1 on v0

--- a/solution.py
+++ b/solution.py
@@ -9,6 +9,21 @@
 KEY_VALUE_HEADS = 8
 HEAD_DIMENSION = 128
 masked_fill_value = -1e30
+
+
+def on_each_block(value, axis, dim, make, out_dim):
+    ways, here, step = (lax.axis_size(axis), lax.axis_index(axis), value.shape[dim])
+    results = []
+    for far in range(ways):
+        arriving = (
+            lax.ppermute(value, axis, [(d, (d + 1) % ways) for d in range(ways)])
+            if far + 1 < ways
+            else value
+        )
+        results.append(make(value, (here - far) % ways * step))
+        value = arriving
+    line = jnp.concatenate(results[::-1], axis=out_dim)
+    return jnp.roll(line, (here + 1) * results[0].shape[out_dim], axis=out_dim)
 
 
 def body(queries, stored_cache_keys, stored_cache_values, out_weight, lengths):
@@ -83,11 +98,14 @@
     own_attention = merged.astype(jnp.bfloat16).reshape(
         REQUEST_COUNT, own_rows, query_heads * HEAD_DIMENSION
     )
-    terms = jnp.einsum(
-        "rnc,cd->rnd",
-        lax.all_gather(own_attention, "blk", axis=1, tiled=True),
-        out_weight,
-        preferred_element_type=jnp.float32,
+    terms = on_each_block(
+        own_attention,
+        "blk",
+        1,
+        lambda own_block, offset: jnp.einsum(
+            "rnc,cd->rnd", own_block, out_weight, preferred_element_type=jnp.float32
+        ),
+        1,
     )
     return lax.psum_scatter(terms, "head", scatter_dimension=1, tiled=True).astype(jnp.bfloat16)
 

time: 83.4 us -> 93.7 us (1.12)
  waiting for transfers between devices: 11 us -> 25 us
  blocking collectives: 38.8 us -> 25.7 us
  matrix products: 13.7 us -> 20.7 us
  local copies, waits for them, and re-layouts: 4.11 us -> 5.49 us
  starting transfers between devices: 13 us -> 14 us
    ppermute x0 -> x3, waiting for transfers between devices: none -> 14 us  [on_each_block(): lax.ppermute(value, axis, [(d, (d + 1) % ways) for d in range(ways)])]
    all_gather x1 -> x0, blocking collectives: 13.1 us -> none  [body(): lax.all_gather(own_attention, 'blk', axis=1, tiled=True)]
    dot_general x1 -> x4, matrix products: 4.71 us -> 11.7 us  [body(): jnp.einsum('rnc,cd->rnd', own_block, out_weight, preferred_element_type=j...]
    unnamed x5 -> x13, local copies, waits for them, and re-layouts: 1.27 us -> 2.55 us
    ppermute x0 -> x3, starting transfers between devices: none -> 0.97 us  [on_each_block(): lax.ppermute(value, axis, [(d, (d + 1) % ways) for d in range(ways)])]
  transfers between devices with their start and end apart: 3 -> 6, of which waited for: 2 -> 5; matrix products, arithmetic and copies ran while one was open for 9% -> 8% of each run, Pallas kernels for 0% -> 0%
where the time goes in v1:
time: 93.7 us; the launch traced here: 93.1 us
  blocking collectives  25.7 us (27%)
  waiting for transfers between devices  25 us (27%)
  matrix products  20.7 us (22%)
  starting transfers between devices  14 us (15%)
  local copies, waits for them, and re-layouts  5.49 us (6%)
  other arithmetic  2.05 us (2%)
    all_gather x1, blocking collectives, body(): piece = lax.all_gather(queries, 'blk', axis=1, tiled=True)  15 us
    ppermute x3, waiting for transfers between devices, on_each_block(): lax.ppermute(value, axis, [(d, (d + 1) % ways) for d in range(ways)])  14 us
    dot_general x4, matrix products, body(): jnp.einsum('rnc,cd->rnd', own_block, out_weight, preferred_element_type=j...  11.7 us
    unnamed x1, blocking collectives  10.7 us
    all_to_all x1, waiting for transfers between devices, body(): lax.all_to_all(new_sums[None], 'blk', split_axis=2, concat_axis=0, tiled=...  5.59 us
    all_to_all x1, waiting for transfers between devices, body(): lax.all_to_all(new_totals[None], 'blk', split_axis=2, concat_axis=0, tile...  5.42 us
    all_to_all x1, starting transfers between devices, body(): lax.all_to_all(new_totals[None], 'blk', split_axis=2, concat_axis=0, tile...  5.09 us
    all_to_all x1, starting transfers between devices, body(): lax.all_to_all(new_maxima[None], 'blk', split_axis=2, concat_axis=0, tile...  4.63 us
  transfers between devices with their start and end apart: 6, of which 5 were waited for; matrix products, arithmetic and copies ran while one was open for 8% of the time, Pallas kernels for 0%

profile of v1, /device:TPU:0, one launch (start us, length us, event | category | flops | bytes accessed | tf_op | source)
XLA Modules:
  0.0 93.1 jit_solution(7944270323710368135)
XLA Ops:
  0.0 0.7 broadcast_add_fusion
  0.7 0.1 iota_add_fusion.1
  0.7 15.0 %all_gather.3 = bf16[2,4,2048]{2,0,1:T(2,128)(2,1)S(1)} all-gather(bf16[2,1,2048]{2,0,1:T(2,128)(2,1)} %param.5), channel_id=1, replica_groups=mesh['groups'=2,'blk'=4,'head'=4] {'blk'}, dimensions={1}, use_global_device_ids=true | all-gather | bytes 40960 | tf_op jit(solution)/shard_map/all_gather | solution.py:37
  15.8 0.1 slice_reduce_fusion.3
  15.9 0.1 broadcast_compare_fusion.1
  16.0 1.1 %select_reduce_fusion.3 = (f32[4,8]{1,0:T(4,128)S(1)}, f32[4,8,512]{2,1,0:T(8,128)S(1)}) fusion(pred[4,512]{1,0:T(4,128)(4,1)S(1)} %get-tuple-element.13, bf16[2,512,256]{2,1,0:T(8,128)(2,1)} %param.6, bf16[1,4,8,128]{3,1,2,0:T(4,128)(2,1)S(1)} %bitcast.186), kind=kOutput, calls=%fused_computation.38 | convolution fusion | flops 4243424 | bytes 206976 | tf_op jit(solution)/shard_map/ngd,cd->ngc/dot_general | solution.py:63
  17.2 1.1 %select_reduce_fusion.1 = (f32[4,8]{1,0:T(4,128)S(1)}, f32[4,8,512]{2,1,0:T(8,128)S(1)}) fusion(pred[4,512]{1,0:T(4,128)(4,1)S(1)} %get-tuple-element.14, bf16[2,512,256]{2,1,0:T(8,128)(2,1)} %param.6, bf16[1,4,8,128]{3,1,2,0:T(4,128)(2,1)S(1)} %bitcast.185), kind=kOutput, calls=%fused_computation.34 | convolution fusion | flops 4243424 | bytes 206976 | tf_op jit(solution)/shard_map/ngd,cd->ngc/dot_general | solution.py:63
  18.3 1.1 %fusion.17 = (f32[4,8]{1,0:T(4,128)S(1)}, f32[4,8]{1,0:T(4,128)S(1)}, f32[4,8,512]{2,1,0:T(8,128)S(1)}) fusion(f32[4,8,512]{2,1,0:T(8,128)S(1)} %get-tuple-element.21, f32[4,8]{1,0:T(4,128)S(1)} %get-tuple-element.20, pred[4,512]{1,0:T(4,128)(4,1)S(1)} %get-tuple-element.13, bf16[2,512,256]{2,1,0:T(8,128)(2,1)} %param.6, ...), kind=kOutput, calls=%fused_computation.39 | convolution fusion | flops 4292544 | bytes 272768 | tf_op jit(solution)/shard_map/ngd,cd->ngc/dot_general | solution.py:63
  19.4 1.1 %fusion.21 = (f32[4,8]{1,0:T(4,128)S(1)}, f32[4,8]{1,0:T(4,128)S(1)}, f32[4,8,512]{2,1,0:T(8,128)S(1)}) fusion(f32[4,8,512]{2,1,0:T(8,128)S(1)} %get-tuple-element.18, f32[4,8]{1,0:T(4,128)S(1)} %get-tuple-element.17, pred[4,512]{1,0:T(4,128)(4,1)S(1)} %get-tuple-element.14, bf16[2,512,256]{2,1,0:T(8,128)(2,1)} %param.6, ...), kind=kOutput, calls=%fused_computation.43 | convolution fusion | flops 4292544 | bytes 272768 | tf_op jit(solution)/shard_map/ngd,cd->ngc/dot_general | solution.py:63
  20.6 0.1 maximum_bitcast_fusion.3
  20.7 0.6 copy.14
  21.3 4.6 %all-to-all-start.1 = ((f32[1,2,4,16]{3,1,0,2:T(2,128)}), f32[1,2,4,16]{3,1,0,2:T(2,128)S(1)}, u32[]{:S(2)}, u32[]{:S(2)}) async-start(f32[1,2,4,16]{3,1,0,2:T(2,128)} %copy.14), calls=%async_computation.1 | async-start | bytes 8192 | tf_op jit(solution)/shard_map/all_to_all | solution.py:87
  25.9 1.1 %convolution_bitcast_fusion.7 = f32[1,4,8,128]{3,2,1,0:T(8,128)S(1)} fusion(bf16[2,512,256]{2,1,0:T(8,128)(2,1)} %param.7, f32[4,8,512]{2,1,0:T(8,128)S(1)} %get-tuple-element.21, f32[4,8]{1,0:T(4,128)S(1)} %get-tuple-element.20, pred[4,512]{1,0:T(4,128)(4,1)S(1)} %get-tuple-element.13), kind=kOutput, calls=%fused_computation.11 | convolution fusion | flops 4243456 | bytes 215168 | tf_op jit(solution)/shard_map/ngc,cd->ngd/dot_general | solution.py:72
  27.0 1.1 %convolution_bitcast_fusion.5 = f32[1,4,8,128]{3,2,1,0:T(8,128)S(1)} fusion(bf16[2,512,256]{2,1,0:T(8,128)(2,1)} %param.7, f32[4,8,512]{2,1,0:T(8,128)S(1)} %get-tuple-element.18, f32[4,8]{1,0:T(4,128)S(1)} %get-tuple-element.17, pred[4,512]{1,0:T(4,128)(4,1)S(1)} %get-tuple-element.14), kind=kOutput, calls=%fused_computation.9 | convolution fusion | flops 4243456 | bytes 215168 | tf_op jit(solution)/shard_map/ngc,cd->ngd/dot_general | solution.py:72
  28.1 1.1 %convolution_bitcast_fusion.6 = f32[1,4,8,128]{3,2,1,0:T(8,128)S(1)} fusion(bf16[2,512,256]{2,1,0:T(8,128)(2,1)} %param.7, f32[4,8,512]{2,1,0:T(8,128)S(1)} %get-tuple-element.22, f32[4,8]{1,0:T(4,128)S(1)} %get-tuple-element.10, pred[4,512]{1,0:T(4,128)(4,1)S(1)} %get-tuple-element.13), kind=kOutput, calls=%fused_computation.10 | convolution fusion | flops 4243456 | bytes 215168 | tf_op jit(solution)/shard_map/ngc,cd->ngd/dot_general | solution.py:72
  29.2 1.1 %convolution_bitcast_fusion.4 = f32[1,4,8,128]{3,2,1,0:T(8,128)S(1)} fusion(bf16[2,512,256]{2,1,0:T(8,128)(2,1)} %param.7, f32[4,8,512]{2,1,0:T(8,128)S(1)} %get-tuple-element.19, f32[4,8]{1,0:T(4,128)S(1)} %get-tuple-element.12, pred[4,512]{1,0:T(4,128)(4,1)S(1)} %get-tuple-element.14), kind=kOutput, calls=%fused_computation.8 | convolution fusion | flops 4243456 | bytes 215168 | tf_op jit(solution)/shard_map/ngc,cd->ngd/dot_general | solution.py:72
  30.3 0.2 fusion.19
  30.7 0.7 maximum_bitcast_fusion
  31.4 0.1 maximum_bitcast_fusion.5
  31.4 0.1 maximum_bitcast_fusion.6
  31.5 0.6 copy.18
  32.1 0.0 all-to-all-done.1
  32.1 5.1 %all-to-all-start.2 = ((f32[1,2,4,16]{3,1,0,2:T(2,128)}), f32[1,2,4,16]{3,1,0,2:T(2,128)S(1)}, u32[]{:S(2)}, u32[]{:S(2)}) async-start(f32[1,2,4,16]{3,1,0,2:T(2,128)} %copy.18), calls=%async_computation.2 | async-start | bytes 8192 | tf_op jit(solution)/shard_map/all_to_all | solution.py:88
  37.2 0.1 mul.44
  37.4 5.4 %all-to-all-done.2 = f32[1,2,4,16]{3,1,0,2:T(2,128)S(1)} async-done(((f32[1,2,4,16]{3,1,0,2:T(2,128)}), f32[1,2,4,16]{3,1,0,2:T(2,128)S(1)}, u32[]{:S(2)}, u32[]{:S(2)}) %all-to-all-start.2) | async-done | bytes 544 | tf_op jit(solution)/shard_map/all_to_all | solution.py:88
  42.8 3.3 %all-to-all-start = ((f32[1,2,4,2048]{3,1,0,2:T(2,128)}), f32[1,2,4,2048]{3,1,0,2:T(2,128)S(1)}, u32[]{:S(2)}, u32[]{:S(2)}) async-start(f32[1,2,4,2048]{3,1,0,2:T(2,128)} %maximum_bitcast_fusion), calls=%async_computation | async-start | bytes 131072 | tf_op jit(solution)/shard_map/all_to_all | solution.py:86
  46.1 0.1 div.24
  46.2 5.6 %all-to-all-done = f32[1,2,4,2048]{3,1,0,2:T(2,128)S(1)} async-done(((f32[1,2,4,2048]{3,1,0,2:T(2,128)}), f32[1,2,4,2048]{3,1,0,2:T(2,128)S(1)}, u32[]{:S(2)}, u32[]{:S(2)}) %all-to-all-start) | async-done | bytes 65568 | tf_op jit(solution)/shard_map/all_to_all | solution.py:86
  51.9 1.0 %collective-permute-start = (bf16[2,1,2048]{2,0,1:T(2,128)(2,1)S(1)}, bf16[2,1,2048]{2,0,1:T(2,128)(2,1)S(1)}, u32[]{:S(2)}, u32[]{:S(2)}) collective-permute-start(bf16[2,1,2048]{2,0,1:T(2,128)(2,1)S(1)} %fusion.41), channel_id=1, source_target_pairs={{0,4},{4,8},{8,12},{12,0},{1,5},{5,9},{9,13},{13,1},{2,6},{6,10},{... | collective-permute-start | bytes 24584 | tf_op jit(solution)/shard_map/ppermute | solution.py:19
  52.8 4.5 %collective-permute-done = bf16[2,1,2048]{2,0,1:T(2,128)(2,1)S(1)} collective-permute-done((bf16[2,1,2048]{2,0,1:T(2,128)(2,1)S(1)}, bf16[2,1,2048]{2,0,1:T(2,128)(2,1)S(1)}, u32[]{:S(2)}, u32[]{:S(2)}) %collective-permute-start) | collective-permute-done | bytes 8224 | tf_op jit(solution)/shard_map/ppermute | solution.py:19
  57.4 0.0 collective-permute-start.1
  57.4 1.3 %dynamic-slice = u32[1]{0:T(128)} dynamic-slice(u32[32]{0:T(128)} %constant.45, u32[]{:T(128)S(6)} %add.49), dynamic_slice_sizes={1} | dynamic-slice | bytes 12
  58.7 4.1 %collective-permute-done.1 = bf16[2,1,2048]{2,0,1:T(2,128)(2,1)S(1)} collective-permute-done((bf16[2,1,2048]{2,0,1:T(2,128)(2,1)S(1)}, bf16[2,1,2048]{2,0,1:T(2,128)(2,1)S(1)}, u32[]{:S(2)}, u32[]{:S(2)}) %collective-permute-start.1) | collective-permute-done | bytes 8224 | tf_op jit(solution)/shard_map/ppermute | solution.py:19
  62.8 0.0 collective-permute-start.2
  62.8 0.1 broadcast_bitcast_fusion
  62.9 5.4 %collective-permute-done.2 = bf16[2,1,2048]{2,0,1:T(2,128)(2,1)S(1)} collective-permute-done((bf16[2,1,2048]{2,0,1:T(2,128)(2,1)S(1)}, bf16[2,1,2048]{2,0,1:T(2,128)(2,1)S(1)}, u32[]{:S(2)}, u32[]{:S(2)}) %collective-permute-start.2) | collective-permute-done | bytes 8224 | tf_op jit(solution)/shard_map/ppermute | solution.py:19
  68.3 4.6 %constant_dynamic-update-slice_fusion.7 = (f32[2,8,2048]{2,0,1:T(2,128)S(1)}, f32[2,1,2048]{2,0,1:T(2,128)S(1)}) fusion(bf16[2048,2048]{1,0:T(8,128)(2,1)} %param.8, bf16[2,1,2048]{2,0,1:T(2,128)(2,1)S(1)} %collective-permute-done.2), kind=kOutput, calls=%fused_computation.68 | convolution fusion | flops 16777215 | bytes 8429568 | tf_op jit(solution)/shard_map/rnc,cd->rnd/dot_general | solution.py:105
  72.8 0.0 slice-start
  72.8 0.0 slice-start.1
  72.8 4.7 %constant_dynamic-update-slice_fusion.6 = (f32[2,8,2048]{2,0,1:T(2,128)S(1)}, f32[2,1,2048]{2,0,1:T(2,128)S(1)}) fusion(f32[2,8,2048]{2,0,1:T(2,128)S(1)} %get-tuple-element.23, bf16[2048,2048]{1,0:T(8,128)(2,1)} %param.8, bf16[2,1,2048]{2,0,1:T(2,128)(2,1)S(1)} %collective-permute-done.1), kind=kOutput, calls=%fused_computation.67 | convolution fusion | flops 16777216 | bytes 8429568 | tf_op jit(solution)/shard_map/rnc,cd->rnd/dot_general | solution.py:105
  77.6 0.0 slice-done
  77.6 1.1 %slice-done.1 = s8[4194304]{0:T(1024)(128)(4,1)S(1)} async-done(((s8[8388608]{0:T(1024)(128)(4,1)}), s8[4194304]{0:T(1024)(128)(4,1)S(1)}, s32[]{:S(2)}) %slice-start.1) | async-done | bytes 4194328
  78.7 1.2 %constant_dynamic-update-slice_fusion.5 = (f32[2,8,2048]{2,0,1:T(2,128)S(1)}, f32[2,1,2048]{2,0,1:T(2,128)S(1)}) fusion(f32[2,8,2048]{2,0,1:T(2,128)S(1)} %get-tuple-element.25, bf16[2048,2048]{1,0:T(8,128)(2,1)S(1)} %bitcast.178, bf16[2,1,2048]{2,0,1:T(2,128)(2,1)S(1)} %collective-permute-done), kind=kOutput, calls=%fused_computation.66 | convolution fusion | flops 16777216 | bytes 8429568 | tf_op jit(solution)/shard_map/rnc,cd->rnd/dot_general | solution.py:105
  79.9 1.2 %constant_dynamic-update-slice_fusion.4 = (f32[2,8,2048]{2,0,1:T(2,128)S(1)}, f32[2,1,2048]{2,0,1:T(2,128)S(1)}) fusion(f32[2,8,2048]{2,0,1:T(2,128)S(1)} %get-tuple-element.27, bf16[2048,2048]{1,0:T(8,128)(2,1)S(1)} %bitcast.178, f32[2,2048]{1,0:T(2,128)S(1)} %fusion.16, f32[1,2,16,128]{3,2,1,0:T(8,128)S(1)} %broadcast_bitcast_fusion), kind=kOutput, calls=%fused_computation.65 | convolution fusion | flops 16785408 | bytes 8454144 | tf_op jit(solution)/shard_map/rnc,cd->rnd/dot_general | solution.py:105
  81.2 10.7 %all-reduce = bf16[2,4,2048]{2,0,1:T(2,128)(2,1)S(1)} all-reduce(f32[2,4,2048]{2,0,1:T(2,128)S(1)} %constant_dynamic-slice_fusion), channel_id=2, replica_groups=mesh['groups'=2,'blk'=4,'head'=4] {'head'}, use_global_device_ids=true, to_apply=%region_11.12.clone | all-reduce | flops 16384 | bytes 98304
  91.8 1.3 %dynamic-slice_convert_fusion = bf16[2,1,2048]{2,0,1:T(2,128)(2,1)} fusion(bf16[2,4,2048]{2,0,1:T(2,128)(2,1)S(1)} %all-reduce, u32[]{:T(128)} %bitcast.45), kind=kLoop, calls=%fused_computation.78 | loop fusion | bytes 16388 | tf_op jit(solution)/shard_map/convert_element_type | solution.py:110
  (27 shorter events, 0.3 us)
Async XLA Ops:
  21.3 10.8 %all-to-all-start.1 = ((f32[1,2,4,16]{3,1,0,2:T(2,128)}), f32[1,2,4,16]{3,1,0,2:T(2,128)S(1)}, u32[]{:S(2)}, u32[]{:S(2)}) async-start(f32[1,2,4,16]{3,1,0,2:T(2,128)} %copy.14), calls=%async_computation.1 | async-start | bytes 8192 | tf_op jit(solution)/shard_map/all_to_all | solution.py:87
  32.1 10.7 %all-to-all-start.2 = ((f32[1,2,4,16]{3,1,0,2:T(2,128)}), f32[1,2,4,16]{3,1,0,2:T(2,128)S(1)}, u32[]{:S(2)}, u32[]{:S(2)}) async-start(f32[1,2,4,16]{3,1,0,2:T(2,128)} %copy.18), calls=%async_computation.2 | async-start | bytes 8192 | tf_op jit(solution)/shard_map/all_to_all | solution.py:88
  42.8 9.0 %all-to-all-start = ((f32[1,2,4,2048]{3,1,0,2:T(2,128)}), f32[1,2,4,2048]{3,1,0,2:T(2,128)S(1)}, u32[]{:S(2)}, u32[]{:S(2)}) async-start(f32[1,2,4,2048]{3,1,0,2:T(2,128)} %maximum_bitcast_fusion), calls=%async_computation | async-start | bytes 131072 | tf_op jit(solution)/shard_map/all_to_all | solution.py:86
  51.9 5.5 %collective-permute-start = (bf16[2,1,2048]{2,0,1:T(2,128)(2,1)S(1)}, bf16[2,1,2048]{2,0,1:T(2,128)(2,1)S(1)}, u32[]{:S(2)}, u32[]{:S(2)}) collective-permute-start(bf16[2,1,2048]{2,0,1:T(2,128)(2,1)S(1)} %fusion.41), channel_id=1, source_target_pairs={{0,4},{4,8},{8,12},{12,0},{1,5},{5,9},{9,13},{13,1},{2,6},{6,10},{... | collective-permute-start | bytes 24584 | tf_op jit(solution)/shard_map/ppermute | solution.py:19
  57.4 5.4 %collective-permute-start.1 = (bf16[2,1,2048]{2,0,1:T(2,128)(2,1)S(1)}, bf16[2,1,2048]{2,0,1:T(2,128)(2,1)S(1)}, u32[]{:S(2)}, u32[]{:S(2)}) collective-permute-start(bf16[2,1,2048]{2,0,1:T(2,128)(2,1)S(1)} %collective-permute-done), channel_id=1, source_target_pairs={{0,4},{4,8},{8,12},{12,0},{1,5},{5,9},{9,13},{13,1},{2,6},{6,10},{... | collective-permute-start | bytes 24584 | tf_op jit(solution)/shard_map/ppermute | solution.py:19
  62.8 5.4 %collective-permute-start.2 = (bf16[2,1,2048]{2,0,1:T(2,128)(2,1)S(1)}, bf16[2,1,2048]{2,0,1:T(2,128)(2,1)S(1)}, u32[]{:S(2)}, u32[]{:S(2)}) collective-permute-start(bf16[2,1,2048]{2,0,1:T(2,128)(2,1)S(1)} %collective-permute-done.1), channel_id=1, source_target_pairs={{0,4},{4,8},{8,12},{12,0},{1,5},{5,9},{9,13},{13,1},{2,6},{6,10},{... | collective-permute-start | bytes 24584 | tf_op jit(solution)/shard_map/ppermute | solution.py:19
  72.8 4.7 %slice-start = ((s8[8388608]{0:T(1024)(128)(4,1)}), s8[4194304]{0:T(1024)(128)(4,1)S(1)}, s32[]{:S(2)}) async-start(s8[8388608]{0:T(1024)(128)(4,1)} %bitcast.177), calls=%async_computation.3 | async-start | bytes 8388608
  72.8 5.9 %slice-start.1 = ((s8[8388608]{0:T(1024)(128)(4,1)}), s8[4194304]{0:T(1024)(128)(4,1)S(1)}, s32[]{:S(2)}) async-start(s8[8388608]{0:T(1024)(128)(4,1)} %bitcast.177), calls=%async_computation.4 | async-start | bytes 8388608
